TPU v7x, 1024 devices: a whole 4x8x16 slice. The times are simulated.
1024 devices in a mesh: rep: 4 (over y_hi), ctx: 32 (over z, y_lo), head: 8 (over x, core).
Axes of the slice: x: 4, y: 8 (y_hi: 4, y_lo: 2; y = y_hi * 2 + y_lo), z: 16, core: 2. Of those that a mesh axis runs over, the one named last changes fastest.
Arguments:
- queries: bfloat16 [98304, 8, 512], P(('rep', 'ctx', 'head')), parts along dimension 0, may hold values from -48 to 48
- keyvals: bfloat16 [98304, 8, 256], P(('rep', 'ctx', 'head')), parts along dimension 0, may hold values from -24 to 24
- doc_lengths: int32 [128], P('rep'), parts along dimension 0, may hold values from 1 to 1536, 24576 in all
Outputs:
- attended: bfloat16 [98304, 8, 512], P(('rep', 'ctx', 'head')), parts along dimension 0
There are 4 independent parts, one for each index of `rep`. A program takes and returns all parts, laid end to end along the dimension named above; each array names one. Nothing has to cross between parts.
Inputs may be any that keep to these rules, and one draw needn't show every extreme that they name: `doc_lengths`: the documents fill the sequence in order and their lengths sum to 24576; one of them is exactly 1536 tokens long.
All inputs are finite; a program needn't handle non-finite values.
Results may differ from a plain program's by a relative error of at most 0.0037.
Values may be sent and summed in bfloat16 or wider, within the bound.
A program may use at most 32 MiB of HBM per device.

v0:
```python
import functools

import jax
import jax.numpy as jnp
from jax import lax
from jax.experimental import pallas as pl
from jax.experimental.pallas import tpu as pltpu
from jax.sharding import PartitionSpec as P

GROUP = 4
HEAD_DIM = 128
REACH = 2
TILE = 128
MASKED = -1e30
LOG2E = 1.4426950408889634
MESH = pl.DeviceIdType.MESH


def spread(step):
    return 4 + (1 - 2 * (step % 2)) * ((step + 1) // 2)


def attention_kernel(
    heads, ctxs, lengths, q_in, kv_in, out, window, q_rows, first_key, scores, mixed,
    kv_send, kv_recv, q_send, q_recv, z_send, z_recv, y_send, y_recv, o_send, o_recv, own_sem,
):
    rows = q_in.shape[1]
    block = heads * rows
    me = lax.axis_index("head")
    ctx = lax.axis_index("ctx")
    odd = ctx % 2
    far = (ctx + 2) % ctxs
    back = (ctx + ctxs - 2) % ctxs
    beside = ctx + 1 - 2 * odd
    span = REACH * block + rows
    tiles = pl.cdiv(span, TILE)
    pad = tiles * TILE - span

    def key_rows(which, piece):
        return window.at[pl.ds(pl.multiple_of(pad + which * block + piece * rows, 32), rows), :]

    def query_rows(piece):
        return q_rows.at[pl.ds(pl.multiple_of(piece * rows, 32), rows), :]

    def kv_copy(dest, source):
        return pltpu.make_async_remote_copy(
            src_ref=kv_in.at[dest], dst_ref=key_rows(REACH, source),
            send_sem=kv_send.at[dest], recv_sem=kv_recv.at[source],
            device_id={"head": dest}, device_id_type=MESH,
        )

    def q_copy(dest, source):
        return pltpu.make_async_remote_copy(
            src_ref=q_in.at[dest], dst_ref=query_rows(source),
            send_sem=q_send.at[dest], recv_sem=q_recv.at[source],
            device_id={"head": dest}, device_id_type=MESH,
        )

    def z_copy(piece):
        return pltpu.make_async_remote_copy(
            src_ref=key_rows(REACH, piece), dst_ref=key_rows(0, piece),
            send_sem=z_send.at[piece], recv_sem=z_recv.at[piece],
            device_id={"ctx": far}, device_id_type=MESH,
        )

    def y_copy(piece):
        return pltpu.make_async_remote_copy(
            src_ref=key_rows(REACH * (1 - odd), piece), dst_ref=key_rows(1, piece),
            send_sem=y_send.at[piece], recv_sem=y_recv.at[piece],
            device_id={"ctx": beside}, device_id_type=MESH,
        )

    def o_copy(dest, source):
        return pltpu.make_async_remote_copy(
            src_ref=mixed.at[dest], dst_ref=out.at[source],
            send_sem=o_send.at[dest], recv_sem=o_recv.at[source],
            device_id={"head": dest}, device_id_type=MESH,
        )

    own_kv = pltpu.make_async_copy(kv_in.at[me], key_rows(REACH, me), own_sem.at[0])
    own_q = pltpu.make_async_copy(q_in.at[me], query_rows(me), own_sem.at[1])
    own_kv.start()
    own_q.start()

    barrier = pltpu.get_barrier_semaphore()
    for step in range(1, heads):
        peer = (me + step) % heads
        pl.semaphore_signal(barrier, inc=1, device_id={"head": peer}, device_id_type=MESH)
    for peer in (far, back, beside):
        pl.semaphore_signal(barrier, inc=1, device_id={"ctx": peer}, device_id_type=MESH)
    pl.semaphore_wait(barrier, heads + 2)

    @pl.loop(0, heads - 1)
    def _(step):
        kv_copy((me + spread(step)) % heads, me).start()

    @pl.loop(0, heads - 1)
    def _(step):
        q_copy((me + spread(step)) % heads, me).start()

    window[:pad, :] = jnp.zeros((pad, window.shape[1]), window.dtype)

    @pl.loop(0, heads)
    def _(chunk):
        place = lax.broadcasted_iota(jnp.int32, (rows, TILE), 0) + (ctx * block + chunk * rows)
        start = jnp.zeros((rows, TILE), jnp.int32)
        end = jnp.int32(0)
        for doc in range(lengths.shape[0]):
            end = end + lengths[doc]
            start = jnp.where(place >= end, end, start)
        first_key[chunk] = start - ((ctx - REACH) * block + chunk * rows - pad)

    own_kv.wait()

    def pass_on(piece):
        z_copy(piece).start()

        @pl.when(odd == 0)
        def _():
            y_copy(piece).start()

    pass_on(me)

    @pl.loop(0, heads - 1)
    def _(step):
        piece = (me + heads - spread(step)) % heads
        kv_copy(piece, piece).wait_recv()
        pass_on(piece)

    @pl.loop(0, heads)
    def _(step):
        piece = (me + heads - spread(heads - 1 - step)) % heads
        z_copy(piece).wait_recv()

        @pl.when(odd == 1)
        def _():
            y_copy(piece).start()

    @pl.loop(0, heads)
    def _(step):
        piece = (me + heads - spread(heads - 1 - step)) % heads
        y_copy(piece).wait_recv()

    own_q.wait()
    sharpness = HEAD_DIM ** -0.5 * LOG2E

    @pl.loop(0, heads)
    def _(step):
        chunk = (me + spread(step)) % heads

        @pl.when(step < heads - 1)
        def _():
            q_copy(chunk, chunk).wait_recv()

        packed = query_rows(chunk)[...]
        stacked = jnp.concatenate(
            [packed[:, j * HEAD_DIM:(j + 1) * HEAD_DIM] for j in range(GROUP)], axis=0
        )
        base = chunk * rows
        lowest = first_key[chunk]
        lane = lax.broadcasted_iota(jnp.int32, (rows, TILE), 1)
        row = lax.broadcasted_iota(jnp.int32, (rows, TILE), 0)
        top = None
        for tile in range(tiles):
            keys = window[pl.ds(pl.multiple_of(base + tile * TILE, 32), TILE), :HEAD_DIM]
            part = lax.dot_general(
                stacked, keys, (((1,), (1,)), ((), ())), preferred_element_type=jnp.float32
            )
            here = lane + tile * TILE
            kept = here >= lowest
            if (tile + 1) * TILE > pad + REACH * block:
                kept = kept & (here <= row + (pad + REACH * block))
            part = jnp.where(kept[None], part.reshape(GROUP, rows, TILE), MASKED)
            part = part.reshape(GROUP * rows, TILE)
            scores[tile] = part
            top = part if top is None else jnp.maximum(top, part)
        top = jnp.max(top, axis=1, keepdims=True)
        total = None
        result = None
        for tile in range(0, tiles, 2):
            weights = []
            for half in range(tile, min(tile + 2, tiles)):
                part = jnp.exp2((scores[half] - top) * sharpness)
                total = part if total is None else total + part
                weights.append(part.astype(jnp.bfloat16))
            weights = jnp.concatenate(weights, axis=1)
            width = weights.shape[1]
            values = window[pl.ds(pl.multiple_of(base + tile * TILE, 32), width), HEAD_DIM:]
            part = jnp.dot(weights, values, preferred_element_type=jnp.float32)
            result = part if result is None else result + part
        total = jnp.sum(total, axis=1, keepdims=True)
        result = (result / total).astype(jnp.bfloat16)
        for j in range(GROUP):
            mixed[chunk, :, j * HEAD_DIM:(j + 1) * HEAD_DIM] = result[j * rows:(j + 1) * rows]

        @pl.when(step < heads - 1)
        def _():
            o_copy(chunk, me).start()

    own_out = pltpu.make_async_copy(mixed.at[me], out.at[me], own_sem.at[2])
    own_out.start()

    @pl.loop(0, heads - 1)
    def _(step):
        dest = (me + spread(step)) % heads
        kv_copy(dest, me).wait_send()
        q_copy(dest, me).wait_send()
        o_copy(dest, me).wait_send()
        o_copy(dest, dest).wait_recv()

    @pl.loop(0, heads)
    def _(piece):
        z_copy(piece).wait_send()
        y_copy(piece).wait_send()

    own_out.wait()


def local(heads, ctxs, queries, keyvals, doc_lengths):
    q_in = jnp.transpose(queries, (1, 0, 2))
    kv_in = jnp.transpose(keyvals, (1, 0, 2))
    rows = queries.shape[0]
    block = heads * rows
    span = REACH * block + rows
    tiles = pl.cdiv(span, TILE)
    pad = tiles * TILE - span
    dma = pltpu.SemaphoreType.DMA((heads,))
    gathered = pl.pallas_call(
        functools.partial(attention_kernel, heads, ctxs),
        out_shape=jax.ShapeDtypeStruct(q_in.shape, jnp.bfloat16),
        in_specs=[
            pl.BlockSpec(memory_space=pltpu.SMEM),
            pl.BlockSpec(memory_space=pl.ANY),
            pl.BlockSpec(memory_space=pl.ANY),
        ],
        out_specs=pl.BlockSpec(memory_space=pl.ANY),
        scratch_shapes=[
            pltpu.VMEM((pad + (REACH + 1) * block, keyvals.shape[2]), jnp.bfloat16),
            pltpu.VMEM((block, queries.shape[2]), jnp.bfloat16),
            pltpu.VMEM((heads, rows, TILE), jnp.int32),
            pltpu.VMEM((tiles, GROUP * rows, TILE), jnp.float32),
            pltpu.VMEM((heads, rows, queries.shape[2]), jnp.bfloat16),
            dma, dma, dma, dma, dma, dma, dma, dma, dma, dma,
            pltpu.SemaphoreType.DMA((3,)),
        ],
        compiler_params=pltpu.CompilerParams(collective_id=0, has_side_effects=True),
    )(doc_lengths, q_in, kv_in)
    return jnp.transpose(gathered, (1, 0, 2))


def solution(mesh):
    spec = P(("rep", "ctx", "head"), None, None)
    return jax.shard_map(
        functools.partial(local, mesh.shape["head"], mesh.shape["ctx"]),
        mesh=mesh,
        in_specs=(spec, spec, P("rep")),
        out_specs=spec,
        check_vma=False,
    )
```

profile of v0, /device:TPU:1, one launch (start us, length us, event | category | flops | bytes accessed | tf_op | source)
XLA Modules:
  0.0 64.2 jit_solution(10743565496737997246)
XLA Ops:
  0.0 0.0 copy-start
  0.0 1.9 %copy.10 = bf16[96,8,256]{2,0,1:T(8,128)(2,1)} copy(bf16[96,8,256]{2,1,0:T(8,128)(2,1)} %param.4) | data formatting | bytes 786432 | tf_op args[1]
  1.9 0.0 copy-done
  1.9 1.1 %copy.9 = bf16[96,8,512]{2,0,1:T(8,128)(2,1)} copy(bf16[96,8,512]{2,1,0:T(8,128)(2,1)S(1)} %copy-done) | data formatting | bytes 1572864 | tf_op args[0]
  3.0 58.8 %shard_map.37 = bf16[8,96,512]{2,1,0:T(8,128)(2,1)} custom-call(s32[32]{0:T(128)} %lengths.1, bf16[8,96,512]{2,1,0:T(8,128)(2,1)} %bitcast.8, bf16[8,96,256]{2,1,0:T(8,128)(2,1)} %bitcast.9), custom_call_target="tpu_custom_call" | custom-call | tf_op jit(solution)/shard_map/pallas_call | solution.py:228
  61.8 2.4 %copy.6 = bf16[96,8,512]{2,1,0:T(8,128)(2,1)} copy(bf16[96,8,512]{2,0,1:T(8,128)(2,1)} %bitcast.7) | data formatting | bytes 1572864 | tf_op jit(solution)/shard_map/transpose | solution.py:248
Async XLA Ops:
  0.0 1.9 %copy-start = (bf16[96,8,512]{2,1,0:T(8,128)(2,1)S(1)}, bf16[96,8,512]{2,1,0:T(8,128)(2,1)}, u32[]{:S(2)}) copy-start(bf16[96,8,512]{2,1,0:T(8,128)(2,1)} %param.3) | copy-start | bytes 2359300
where the time goes:
time: 64.4 us; the launch traced here: 64.2 us
  Pallas kernels  58.8 us (91%)
  local copies, waits for them, and re-layouts  5.45 us (8%)
    pallas_call x1, Pallas kernels, local(): pl.pallas_call(functools.partial(attention_kernel, heads, ctxs), out_shap...  58.8 us
    unnamed x4, local copies, waits for them, and re-layouts  3 us
    transpose x1, local copies, waits for them, and re-layouts, local(): return jnp.transpose(gathered, (1, 0, 2))  2.45 us

commit v1 on v0

--- a/solution.py
+++ b/solution.py
@@ -16,12 +16,19 @@
 MESH = pl.DeviceIdType.MESH
 
 
-def spread(step):
-    return 4 + (1 - 2 * (step % 2)) * ((step + 1) // 2)
+NEAR_FIRST = (6, 3, 5, 2, 4, 1, 0)
+
+
+def peer_at(me, step, heads, way):
+    pair = step // 2
+    chips = heads // 2
+    distance = chips // 2 + (1 - 2 * (pair % 2)) * ((pair + 1) // 2)
+    flip = (step + pair // 3) % 2
+    return 2 * ((me // 2 + chips + way * distance) % chips) + (me + flip) % 2
 
 
 def attention_kernel(
-    heads, ctxs, lengths, q_in, kv_in, out, window, q_rows, first_key, scores, mixed,
+    heads, ctxs, doc_lengths, q_in, kv_in, out, window, q_rows, lengths, first_key, scores_a, scores_b, tops, mixed,
     kv_send, kv_recv, q_send, q_recv, z_send, z_recv, y_send, y_recv, o_send, o_recv, own_sem,
 ):
     rows = q_in.shape[1]
@@ -79,6 +86,8 @@
 
     own_kv = pltpu.make_async_copy(kv_in.at[me], key_rows(REACH, me), own_sem.at[0])
     own_q = pltpu.make_async_copy(q_in.at[me], query_rows(me), own_sem.at[1])
+    lengths_in = pltpu.make_async_copy(doc_lengths, lengths, own_sem.at[3])
+    lengths_in.start()
     own_kv.start()
     own_q.start()
 
@@ -86,19 +95,20 @@
     for step in range(1, heads):
         peer = (me + step) % heads
         pl.semaphore_signal(barrier, inc=1, device_id={"head": peer}, device_id_type=MESH)
-    for peer in (far, back, beside):
+    for peer in (back, beside):
         pl.semaphore_signal(barrier, inc=1, device_id={"ctx": peer}, device_id_type=MESH)
-    pl.semaphore_wait(barrier, heads + 2)
+    pl.semaphore_wait(barrier, heads + 1)
+
+    for step in NEAR_FIRST:
+        kv_copy(peer_at(me, step, heads, 1), me).start()
 
     @pl.loop(0, heads - 1)
     def _(step):
-        kv_copy((me + spread(step)) % heads, me).start()
-
-    @pl.loop(0, heads - 1)
-    def _(step):
-        q_copy((me + spread(step)) % heads, me).start()
+        q_copy(peer_at(me, step, heads, 1), me).start()
 
     window[:pad, :] = jnp.zeros((pad, window.shape[1]), window.dtype)
+
+    lengths_in.wait()
 
     @pl.loop(0, heads)
     def _(chunk):
@@ -120,38 +130,30 @@
             y_copy(piece).start()
 
     pass_on(me)
-
-    @pl.loop(0, heads - 1)
-    def _(step):
-        piece = (me + heads - spread(step)) % heads
+    for step in NEAR_FIRST:
+        piece = peer_at(me, step, heads, -1)
         kv_copy(piece, piece).wait_recv()
         pass_on(piece)
 
+    for step in (heads - 1, *NEAR_FIRST):
+        piece = peer_at(me, step, heads, -1)
+        z_copy(piece).wait_recv()
+
+        @pl.when(odd == 1)
+        def _():
+            y_copy(piece).start()
+
     @pl.loop(0, heads)
-    def _(step):
-        piece = (me + heads - spread(heads - 1 - step)) % heads
-        z_copy(piece).wait_recv()
-
-        @pl.when(odd == 1)
-        def _():
-            y_copy(piece).start()
-
-    @pl.loop(0, heads)
-    def _(step):
-        piece = (me + heads - spread(heads - 1 - step)) % heads
+    def _(piece):
         y_copy(piece).wait_recv()
 
     own_q.wait()
     sharpness = HEAD_DIM ** -0.5 * LOG2E
 
-    @pl.loop(0, heads)
-    def _(step):
-        chunk = (me + spread(step)) % heads
-
-        @pl.when(step < heads - 1)
-        def _():
-            q_copy(chunk, chunk).wait_recv()
-
+    def chunk_of(step):
+        return peer_at(me, step, heads, 1)
+
+    def score(chunk, scores):
         packed = query_rows(chunk)[...]
         stacked = jnp.concatenate(
             [packed[:, j * HEAD_DIM:(j + 1) * HEAD_DIM] for j in range(GROUP)], axis=0
@@ -161,48 +163,73 @@
         lane = lax.broadcasted_iota(jnp.int32, (rows, TILE), 1)
         row = lax.broadcasted_iota(jnp.int32, (rows, TILE), 0)
         top = None
-        for tile in range(tiles):
-            keys = window[pl.ds(pl.multiple_of(base + tile * TILE, 32), TILE), :HEAD_DIM]
-            part = lax.dot_general(
+        for tile in range(0, tiles, 2):
+            width = min(2, tiles - tile) * TILE
+            keys = window[pl.ds(pl.multiple_of(base + tile * TILE, 32), width), :HEAD_DIM]
+            both = lax.dot_general(
                 stacked, keys, (((1,), (1,)), ((), ())), preferred_element_type=jnp.float32
             )
-            here = lane + tile * TILE
-            kept = here >= lowest
-            if (tile + 1) * TILE > pad + REACH * block:
-                kept = kept & (here <= row + (pad + REACH * block))
-            part = jnp.where(kept[None], part.reshape(GROUP, rows, TILE), MASKED)
-            part = part.reshape(GROUP * rows, TILE)
-            scores[tile] = part
-            top = part if top is None else jnp.maximum(top, part)
-        top = jnp.max(top, axis=1, keepdims=True)
+            for half in range(width // TILE):
+                part = both[:, half * TILE:(half + 1) * TILE]
+                here = lane + (tile + half) * TILE
+                kept = here >= lowest
+                if (tile + half + 1) * TILE > pad + REACH * block:
+                    kept = kept & (here <= row + (pad + REACH * block))
+                part = jnp.where(kept[None], part.reshape(GROUP, rows, TILE), MASKED)
+                part = part.reshape(GROUP * rows, TILE)
+                scores[tile + half] = part
+                top = part if top is None else jnp.maximum(top, part)
+        return jnp.max(top, axis=1, keepdims=True)
+
+    def mix(chunk, scores, top):
+        base = chunk * rows
         total = None
-        result = None
-        for tile in range(0, tiles, 2):
-            weights = []
-            for half in range(tile, min(tile + 2, tiles)):
-                part = jnp.exp2((scores[half] - top) * sharpness)
-                total = part if total is None else total + part
-                weights.append(part.astype(jnp.bfloat16))
-            weights = jnp.concatenate(weights, axis=1)
-            width = weights.shape[1]
-            values = window[pl.ds(pl.multiple_of(base + tile * TILE, 32), width), HEAD_DIM:]
-            part = jnp.dot(weights, values, preferred_element_type=jnp.float32)
-            result = part if result is None else result + part
+        weights = []
+        for tile in range(tiles):
+            part = jnp.exp2((scores[tile] - top) * sharpness)
+            total = part if total is None else total + part
+            weights.append(part.astype(jnp.bfloat16))
+        values = window[pl.ds(pl.multiple_of(base, 32), tiles * TILE), HEAD_DIM:]
+        result = jnp.dot(
+            jnp.concatenate(weights, axis=1), values, preferred_element_type=jnp.float32
+        )
         total = jnp.sum(total, axis=1, keepdims=True)
         result = (result / total).astype(jnp.bfloat16)
         for j in range(GROUP):
             mixed[chunk, :, j * HEAD_DIM:(j + 1) * HEAD_DIM] = result[j * rows:(j + 1) * rows]
 
+    def await_queries(step):
         @pl.when(step < heads - 1)
         def _():
-            o_copy(chunk, me).start()
+            source = chunk_of(step)
+            q_copy(source, source).wait_recv()
+
+    def send_mixed(step):
+        @pl.when(step < heads - 1)
+        def _():
+            o_copy(chunk_of(step), me).start()
+
+    await_queries(0)
+    tops[0] = score(chunk_of(0), scores_a)
+
+    @pl.loop(0, heads, step=2)
+    def _(step):
+        await_queries(step + 1)
+        tops[1] = score(chunk_of(step + 1), scores_b)
+        mix(chunk_of(step), scores_a, tops[0])
+        send_mixed(step)
+        after = jnp.minimum(step + 2, heads - 1)
+        await_queries(step + 2)
+        tops[0] = score(chunk_of(after), scores_a)
+        mix(chunk_of(step + 1), scores_b, tops[1])
+        send_mixed(step + 1)
 
     own_out = pltpu.make_async_copy(mixed.at[me], out.at[me], own_sem.at[2])
     own_out.start()
 
     @pl.loop(0, heads - 1)
     def _(step):
-        dest = (me + spread(step)) % heads
+        dest = (me + 1 + step) % heads
         kv_copy(dest, me).wait_send()
         q_copy(dest, me).wait_send()
         o_copy(dest, me).wait_send()
@@ -229,7 +256,7 @@
         functools.partial(attention_kernel, heads, ctxs),
         out_shape=jax.ShapeDtypeStruct(q_in.shape, jnp.bfloat16),
         in_specs=[
-            pl.BlockSpec(memory_space=pltpu.SMEM),
+            pl.BlockSpec(memory_space=pltpu.HBM),
             pl.BlockSpec(memory_space=pl.ANY),
             pl.BlockSpec(memory_space=pl.ANY),
         ],
@@ -237,14 +264,17 @@
         scratch_shapes=[
             pltpu.VMEM((pad + (REACH + 1) * block, keyvals.shape[2]), jnp.bfloat16),
             pltpu.VMEM((block, queries.shape[2]), jnp.bfloat16),
+            pltpu.SMEM(doc_lengths.shape, jnp.int32),
             pltpu.VMEM((heads, rows, TILE), jnp.int32),
             pltpu.VMEM((tiles, GROUP * rows, TILE), jnp.float32),
+            pltpu.VMEM((tiles, GROUP * rows, TILE), jnp.float32),
+            pltpu.VMEM((2, GROUP * rows, 1), jnp.float32),
             pltpu.VMEM((heads, rows, queries.shape[2]), jnp.bfloat16),
             dma, dma, dma, dma, dma, dma, dma, dma, dma, dma,
-            pltpu.SemaphoreType.DMA((3,)),
+            pltpu.SemaphoreType.DMA((4,)),
         ],
-        compiler_params=pltpu.CompilerParams(collective_id=0, has_side_effects=True),
-    )(doc_lengths, q_in, kv_in)
+        compiler_params=pltpu.CompilerParams(collective_id=0, has_side_effects=True, vmem_limit_bytes=20 << 20),
+    )(pltpu.with_memory_space_constraint(doc_lengths, pltpu.HBM), q_in, kv_in)
     return jnp.transpose(gathered, (1, 0, 2))
 
 

time: 64.4 us -> 53.3 us (0.83)
  Pallas kernels: 58.8 us -> 50.3 us
  local copies, waits for them, and re-layouts: 5.45 us -> 2.79 us
    pallas_call x1, Pallas kernels: 58.8 us -> 50.3 us  [local(): pl.pallas_call(functools.partial(attention_kernel, heads, ctxs), out_shap...]
    unnamed x4, local copies, waits for them, and re-layouts: 3 us -> 1.48 us
    transpose x1, local copies, waits for them, and re-layouts: 2.45 us -> 1.31 us  [local(): return jnp.transpose(gathered, (1, 0, 2))]
where the time goes in v1:
time: 53.3 us; the launch traced here: 53.1 us
  Pallas kernels  50.3 us (94%)
  local copies, waits for them, and re-layouts  2.79 us (5%)
    pallas_call x1, Pallas kernels, local(): pl.pallas_call(functools.partial(attention_kernel, heads, ctxs), out_shap...  50.3 us
    unnamed x4, local copies, waits for them, and re-layouts  1.48 us
    transpose x1, local copies, waits for them, and re-layouts, local(): return jnp.transpose(gathered, (1, 0, 2))  1.31 us

profile of v1, /device:TPU:1, one launch (start us, length us, event | category | flops | bytes accessed | tf_op | source)
XLA Modules:
  0.0 53.1 jit_solution(2101923070329802712)
XLA Ops:
  0.0 0.0 copy-start
  0.0 1.1 %copy.10 = bf16[96,8,256]{2,0,1:T(8,128)(2,1)S(1)} copy(bf16[96,8,256]{2,1,0:T(8,128)(2,1)} %param.4) | data formatting | bytes 786432 | tf_op args[1]
  1.2 0.1 copy-done
  1.3 0.2 copy.9
  1.5 50.3 %shard_map.37 = bf16[8,96,512]{2,1,0:T(8,128)(2,1)S(1)} custom-call(s32[32]{0:T(128)} %doc_lengths.1, bf16[8,96,512]{2,1,0:T(8,128)(2,1)S(1)} %bitcast.8, bf16[8,96,256]{2,1,0:T(8,128)(2,1)S(1)} %bitcast.9), custom_call_target="tpu_custom_call" | custom-call | tf_op jit(solution)/shard_map/pallas_call | solution.py:255
  51.8 1.3 %copy.6 = bf16[96,8,512]{2,1,0:T(8,128)(2,1)} copy(bf16[96,8,512]{2,0,1:T(8,128)(2,1)S(1)} %bitcast.7) | data formatting | bytes 1572864 | tf_op jit(solution)/shard_map/transpose | solution.py:278
Async XLA Ops:
  0.0 1.3 %copy-start = (bf16[96,8,512]{2,1,0:T(8,128)(2,1)S(1)}, bf16[96,8,512]{2,1,0:T(8,128)(2,1)}, u32[]{:S(2)}) copy-start(bf16[96,8,512]{2,1,0:T(8,128)(2,1)} %param.3) | copy-start | bytes 2359300

commit v2 on v1

--- a/solution.py
+++ b/solution.py
@@ -36,8 +36,10 @@
     me = lax.axis_index("head")
     ctx = lax.axis_index("ctx")
     odd = ctx % 2
-    far = (ctx + 2) % ctxs
-    back = (ctx + ctxs - 2) % ctxs
+    first = ctx < REACH
+    last = ctx >= ctxs - REACH
+    far = (ctx + REACH) % ctxs
+    back = (ctx + ctxs - REACH) % ctxs
     beside = ctx + 1 - 2 * odd
     span = REACH * block + rows
     tiles = pl.cdiv(span, TILE)
@@ -95,9 +97,25 @@
     for step in range(1, heads):
         peer = (me + step) % heads
         pl.semaphore_signal(barrier, inc=1, device_id={"head": peer}, device_id_type=MESH)
-    for peer in (back, beside):
-        pl.semaphore_signal(barrier, inc=1, device_id={"ctx": peer}, device_id_type=MESH)
-    pl.semaphore_wait(barrier, heads + 1)
+    pl.semaphore_signal(barrier, inc=1, device_id={"ctx": beside}, device_id_type=MESH)
+
+    @pl.when(jnp.logical_not(first))
+    def _():
+        pl.semaphore_signal(barrier, inc=1, device_id={"ctx": back}, device_id_type=MESH)
+
+    window[:pad, :] = jnp.zeros((pad, window.shape[1]), window.dtype)
+
+    @pl.when(first)
+    def _():
+        window[pad:pad + block, :] = jnp.zeros((block, window.shape[1]), window.dtype)
+
+    @pl.when(ctx == 0)
+    def _():
+        window[pad + block:pad + REACH * block, :] = jnp.zeros(
+            (block, window.shape[1]), window.dtype
+        )
+
+    pl.semaphore_wait(barrier, heads + 1 - (ctx + REACH) // ctxs)
 
     for step in NEAR_FIRST:
         kv_copy(peer_at(me, step, heads, 1), me).start()
@@ -105,8 +123,6 @@
     @pl.loop(0, heads - 1)
     def _(step):
         q_copy(peer_at(me, step, heads, 1), me).start()
-
-    window[:pad, :] = jnp.zeros((pad, window.shape[1]), window.dtype)
 
     lengths_in.wait()
 
@@ -123,7 +139,9 @@
     own_kv.wait()
 
     def pass_on(piece):
-        z_copy(piece).start()
+        @pl.when(jnp.logical_not(last))
+        def _():
+            z_copy(piece).start()
 
         @pl.when(odd == 0)
         def _():
@@ -135,17 +153,21 @@
         kv_copy(piece, piece).wait_recv()
         pass_on(piece)
 
-    for step in (heads - 1, *NEAR_FIRST):
-        piece = peer_at(me, step, heads, -1)
-        z_copy(piece).wait_recv()
-
-        @pl.when(odd == 1)
-        def _():
-            y_copy(piece).start()
-
-    @pl.loop(0, heads)
-    def _(piece):
-        y_copy(piece).wait_recv()
+    @pl.when(jnp.logical_not(first))
+    def _():
+        for step in (heads - 1, *NEAR_FIRST):
+            piece = peer_at(me, step, heads, -1)
+            z_copy(piece).wait_recv()
+
+            @pl.when(odd == 1)
+            def _():
+                y_copy(piece).start()
+
+    @pl.when(ctx >= 1)
+    def _():
+        @pl.loop(0, heads)
+        def _(piece):
+            y_copy(piece).wait_recv()
 
     own_q.wait()
     sharpness = HEAD_DIM ** -0.5 * LOG2E
@@ -235,10 +257,17 @@
         o_copy(dest, me).wait_send()
         o_copy(dest, dest).wait_recv()
 
-    @pl.loop(0, heads)
-    def _(piece):
-        z_copy(piece).wait_send()
-        y_copy(piece).wait_send()
+    @pl.when(jnp.logical_not(last))
+    def _():
+        @pl.loop(0, heads)
+        def _(piece):
+            z_copy(piece).wait_send()
+
+    @pl.when(ctx != 1)
+    def _():
+        @pl.loop(0, heads)
+        def _(piece):
+            y_copy(piece).wait_send()
 
     own_out.wait()
 

time: 53.3 us -> 45 us (0.84)
  the two profiles are of different devices: /device:TPU:1 before, /device:TPU:15 now
where the time goes in v2:
time: 45 us; the launch traced here: 44.9 us
  Pallas kernels  42.1 us (94%)
  local copies, waits for them, and re-layouts  2.79 us (6%)
    pallas_call x1, Pallas kernels, local(): pl.pallas_call(functools.partial(attention_kernel, heads, ctxs), out_shap...  42.1 us
    unnamed x4, local copies, waits for them, and re-layouts  1.48 us
    transpose x1, local copies, waits for them, and re-layouts, local(): return jnp.transpose(gathered, (1, 0, 2))  1.31 us

profile of v2, /device:TPU:15, one launch (start us, length us, event | category | flops | bytes accessed | tf_op | source)
XLA Modules:
  0.0 44.9 jit_solution(10946465383917248829)
XLA Ops:
  0.0 0.0 copy-start
  0.0 1.1 %copy.10 = bf16[96,8,256]{2,0,1:T(8,128)(2,1)S(1)} copy(bf16[96,8,256]{2,1,0:T(8,128)(2,1)} %param.4) | data formatting | bytes 786432 | tf_op args[1]
  1.2 0.1 copy-done
  1.3 0.2 copy.9
  1.5 42.1 %shard_map.37 = bf16[8,96,512]{2,1,0:T(8,128)(2,1)S(1)} custom-call(s32[32]{0:T(128)} %doc_lengths.1, bf16[8,96,512]{2,1,0:T(8,128)(2,1)S(1)} %bitcast.8, bf16[8,96,256]{2,1,0:T(8,128)(2,1)S(1)} %bitcast.9), custom_call_target="tpu_custom_call" | custom-call | tf_op jit(solution)/shard_map/pallas_call | solution.py:284
  43.6 1.3 %copy.6 = bf16[96,8,512]{2,1,0:T(8,128)(2,1)} copy(bf16[96,8,512]{2,0,1:T(8,128)(2,1)S(1)} %bitcast.7) | data formatting | bytes 1572864 | tf_op jit(solution)/shard_map/transpose | solution.py:307
Async XLA Ops:
  0.0 1.3 %copy-start = (bf16[96,8,512]{2,1,0:T(8,128)(2,1)S(1)}, bf16[96,8,512]{2,1,0:T(8,128)(2,1)}, u32[]{:S(2)}) copy-start(bf16[96,8,512]{2,1,0:T(8,128)(2,1)} %param.3) | copy-start | bytes 2359300

commit v3 on v2

--- a/solution.py
+++ b/solution.py
@@ -28,7 +28,7 @@
 
 
 def attention_kernel(
-    heads, ctxs, doc_lengths, q_in, kv_in, out, window, q_rows, lengths, first_key, scores_a, scores_b, tops, mixed,
+    heads, ctxs, doc_lengths, q_hbm, kv_hbm, out, q_raw, kv_raw, q_in, kv_in, window, q_rows, lengths, first_key, scores_a, scores_b, tops, mixed,
     kv_send, kv_recv, q_send, q_recv, z_send, z_recv, y_send, y_recv, o_send, o_recv, own_sem,
 ):
     rows = q_in.shape[1]
@@ -89,15 +89,20 @@
     own_kv = pltpu.make_async_copy(kv_in.at[me], key_rows(REACH, me), own_sem.at[0])
     own_q = pltpu.make_async_copy(q_in.at[me], query_rows(me), own_sem.at[1])
     lengths_in = pltpu.make_async_copy(doc_lengths, lengths, own_sem.at[3])
+    kv_load = pltpu.make_async_copy(kv_hbm, kv_raw, own_sem.at[4])
+    q_load = pltpu.make_async_copy(q_hbm, q_raw, own_sem.at[5])
+    kv_load.start()
+    q_load.start()
     lengths_in.start()
-    own_kv.start()
-    own_q.start()
 
     barrier = pltpu.get_barrier_semaphore()
     for step in range(1, heads):
         peer = (me + step) % heads
         pl.semaphore_signal(barrier, inc=1, device_id={"head": peer}, device_id_type=MESH)
-    pl.semaphore_signal(barrier, inc=1, device_id={"ctx": beside}, device_id_type=MESH)
+
+    @pl.when(ctx != 0)
+    def _():
+        pl.semaphore_signal(barrier, inc=1, device_id={"ctx": beside}, device_id_type=MESH)
 
     @pl.when(jnp.logical_not(first))
     def _():
@@ -115,10 +120,19 @@
             (block, window.shape[1]), window.dtype
         )
 
-    pl.semaphore_wait(barrier, heads + 1 - (ctx + REACH) // ctxs)
+    onward = 1 - (ctx + REACH) // ctxs
+    across = ((ctx + ctxs - 1) % ctxs + ctxs - 1) // ctxs
+    kv_load.wait()
+    kv_in[...] = jnp.swapaxes(kv_raw[...], 0, 1)
+    own_kv.start()
+    pl.semaphore_wait(barrier, heads - 1 + onward + across)
 
     for step in NEAR_FIRST:
         kv_copy(peer_at(me, step, heads, 1), me).start()
+
+    q_load.wait()
+    q_in[...] = jnp.swapaxes(q_raw[...], 0, 1)
+    own_q.start()
 
     @pl.loop(0, heads - 1)
     def _(step):
@@ -273,8 +287,6 @@
 
 
 def local(heads, ctxs, queries, keyvals, doc_lengths):
-    q_in = jnp.transpose(queries, (1, 0, 2))
-    kv_in = jnp.transpose(keyvals, (1, 0, 2))
     rows = queries.shape[0]
     block = heads * rows
     span = REACH * block + rows
@@ -283,14 +295,18 @@
     dma = pltpu.SemaphoreType.DMA((heads,))
     gathered = pl.pallas_call(
         functools.partial(attention_kernel, heads, ctxs),
-        out_shape=jax.ShapeDtypeStruct(q_in.shape, jnp.bfloat16),
+        out_shape=jax.ShapeDtypeStruct((heads, rows, queries.shape[2]), jnp.bfloat16),
         in_specs=[
             pl.BlockSpec(memory_space=pltpu.HBM),
-            pl.BlockSpec(memory_space=pl.ANY),
-            pl.BlockSpec(memory_space=pl.ANY),
+            pl.BlockSpec(memory_space=pltpu.HBM),
+            pl.BlockSpec(memory_space=pltpu.HBM),
         ],
         out_specs=pl.BlockSpec(memory_space=pl.ANY),
         scratch_shapes=[
+            pltpu.VMEM(queries.shape, jnp.bfloat16),
+            pltpu.VMEM(keyvals.shape, jnp.bfloat16),
+            pltpu.VMEM((heads, rows, queries.shape[2]), jnp.bfloat16),
+            pltpu.VMEM((heads, rows, keyvals.shape[2]), jnp.bfloat16),
             pltpu.VMEM((pad + (REACH + 1) * block, keyvals.shape[2]), jnp.bfloat16),
             pltpu.VMEM((block, queries.shape[2]), jnp.bfloat16),
             pltpu.SMEM(doc_lengths.shape, jnp.int32),
@@ -300,10 +316,10 @@
             pltpu.VMEM((2, GROUP * rows, 1), jnp.float32),
             pltpu.VMEM((heads, rows, queries.shape[2]), jnp.bfloat16),
             dma, dma, dma, dma, dma, dma, dma, dma, dma, dma,
-            pltpu.SemaphoreType.DMA((4,)),
+            pltpu.SemaphoreType.DMA((6,)),
         ],
         compiler_params=pltpu.CompilerParams(collective_id=0, has_side_effects=True, vmem_limit_bytes=20 << 20),
-    )(pltpu.with_memory_space_constraint(doc_lengths, pltpu.HBM), q_in, kv_in)
+    )(*(pltpu.with_memory_space_constraint(x, pltpu.HBM) for x in (doc_lengths, queries, keyvals)))
     return jnp.transpose(gathered, (1, 0, 2))
 
 

time: 45 us -> 43.4 us (0.964)
  local copies, waits for them, and re-layouts: 2.79 us -> 1.31 us
    unnamed x4 -> x0, local copies, waits for them, and re-layouts: 1.48 us -> none
where the time goes in v3:
time: 43.4 us; the launch traced here: 43.2 us
  Pallas kernels  41.9 us (97%)
  local copies, waits for them, and re-layouts  1.31 us (3%)
    pallas_call x1, Pallas kernels, local(): pl.pallas_call(functools.partial(attention_kernel, heads, ctxs), out_shap...  41.9 us
    transpose x1, local copies, waits for them, and re-layouts, local(): return jnp.transpose(gathered, (1, 0, 2))  1.31 us

profile of v3, /device:TPU:15, one launch (start us, length us, event | category | flops | bytes accessed | tf_op | source)
XLA Modules:
  0.0 43.2 jit_solution(3500407151354046263)
XLA Ops:
  0.0 41.9 %shard_map.37 = bf16[8,96,512]{2,1,0:T(8,128)(2,1)S(1)} custom-call(s32[32]{0:T(128)} %doc_lengths.1, bf16[96,8,512]{2,1,0:T(8,128)(2,1)} %q_hbm.1, bf16[96,8,256]{2,1,0:T(8,128)(2,1)} %kv_hbm.1), custom_call_target="tpu_custom_call" | custom-call | tf_op jit(solution)/shard_map/pallas_call | solution.py:296
  41.9 1.3 %copy.4 = bf16[96,8,512]{2,1,0:T(8,128)(2,1)} copy(bf16[96,8,512]{2,0,1:T(8,128)(2,1)S(1)} %bitcast.1) | data formatting | bytes 1572864 | tf_op jit(solution)/shard_map/transpose | solution.py:323

commit v4 on v3

--- a/solution.py
+++ b/solution.py
@@ -130,6 +130,19 @@
     for step in NEAR_FIRST:
         kv_copy(peer_at(me, step, heads, 1), me).start()
 
+    own_kv.wait()
+
+    def pass_on(piece):
+        @pl.when(jnp.logical_not(last))
+        def _():
+            z_copy(piece).start()
+
+        @pl.when(odd == 0)
+        def _():
+            y_copy(piece).start()
+
+    pass_on(me)
+
     q_load.wait()
     q_in[...] = jnp.swapaxes(q_raw[...], 0, 1)
     own_q.start()
@@ -150,18 +163,6 @@
             start = jnp.where(place >= end, end, start)
         first_key[chunk] = start - ((ctx - REACH) * block + chunk * rows - pad)
 
-    own_kv.wait()
-
-    def pass_on(piece):
-        @pl.when(jnp.logical_not(last))
-        def _():
-            z_copy(piece).start()
-
-        @pl.when(odd == 0)
-        def _():
-            y_copy(piece).start()
-
-    pass_on(me)
     for step in NEAR_FIRST:
         piece = peer_at(me, step, heads, -1)
         kv_copy(piece, piece).wait_recv()

time: 43.4 us -> 43.4 us (level)
  no operation moved by 1% of the time
where the time goes in v4:
time: 43.4 us; the launch traced here: 43.2 us
  Pallas kernels  41.9 us (97%)
  local copies, waits for them, and re-layouts  1.31 us (3%)
    pallas_call x1, Pallas kernels, local(): pl.pallas_call(functools.partial(attention_kernel, heads, ctxs), out_shap...  41.9 us
    transpose x1, local copies, waits for them, and re-layouts, local(): return jnp.transpose(gathered, (1, 0, 2))  1.31 us

profile of v4, /device:TPU:15, one launch (start us, length us, event | category | flops | bytes accessed | tf_op | source)
XLA Modules:
  0.0 43.2 jit_solution(16354782067212079241)
XLA Ops:
  0.0 41.9 %shard_map.37 = bf16[8,96,512]{2,1,0:T(8,128)(2,1)S(1)} custom-call(s32[32]{0:T(128)} %doc_lengths.1, bf16[96,8,512]{2,1,0:T(8,128)(2,1)} %q_hbm.1, bf16[96,8,256]{2,1,0:T(8,128)(2,1)} %kv_hbm.1), custom_call_target="tpu_custom_call" | custom-call | tf_op jit(solution)/shard_map/pallas_call | solution.py:297
  41.9 1.3 %copy.4 = bf16[96,8,512]{2,1,0:T(8,128)(2,1)} copy(bf16[96,8,512]{2,0,1:T(8,128)(2,1)S(1)} %bitcast.1) | data formatting | bytes 1572864 | tf_op jit(solution)/shard_map/transpose | solution.py:324
